TPU v7x, 32 devices: a whole 2x2x4 slice. The times are simulated.
32 devices in a mesh: context: 4 (over z), dp: 4 (over y, x), tensor: 2 (over core).
Axes of the slice: x: 2, y: 2, z: 4, core: 2. Of those that a mesh axis runs over, the one named last changes fastest.
Arguments:
- ssm_input: bfloat16 [4096, 4096], P(('dp', 'context'), 'tensor'), parts along dimension 0, may hold values from -6 to 6
- input_map: bfloat16 [4096, 128], P(('dp', 'context')), parts along dimension 0, may hold values from -0.119628906 to 0.119628906
- output_map: bfloat16 [4096, 128], P(('dp', 'context')), parts along dimension 0, may hold values from -6 to 6
- step_size: float32 [64, 4096], P('tensor', ('dp', 'context')), parts along dimension 1, may hold values from 0.25 to 1
- log_decay: float32 [64, 4096], P('tensor', ('dp', 'context')), parts along dimension 1, may hold values from -1.6 to 0
- skip_gain: float32 [64], P('tensor'), may hold values from 0.5 to 1.5
- norm_gain: float32 [4096], P('tensor'), may hold values from 0.5 to 1.5
- query_weight: bfloat16 [4096, 4096], P('tensor'), may hold values from -0.09375 to 0.09375
- key_states: bfloat16 [4096, 1024], P(('dp', 'context'), 'tensor'), parts along dimension 0, may hold values from -140 to 140
- value_states: bfloat16 [4096, 1024], P(('dp', 'context'), 'tensor'), parts along dimension 0, may hold values from -6 to 6
- block_mask: int32 [32, 8], P('dp'), parts along dimension 0, may hold values 0 or 1
Outputs:
- mixer_out: bfloat16 [4096, 4096], P(('dp', 'context'), 'tensor'), parts along dimension 0
- attended: bfloat16 [4096, 4096], P(('dp', 'context'), 'tensor'), parts along dimension 0
There are 4 independent parts, one for each index of `dp`. A program takes and returns all parts, laid end to end along the dimension named above; an argument that names none is the same for every part. Nothing has to cross between parts.
All inputs are finite; a program needn't handle non-finite values.
Results may differ from a plain program's by a relative error of at most 0.0045.
The roundings to bfloat16 on the way count: a program that leaves them out, or rounds other values in their place, can miss the bound.
Values may be sent and summed in bfloat16 or wider, within the bound.
A program may use at most 128 MiB of HBM per device.

v0:
```python
import math

import jax
import jax.numpy as jnp
from jax import lax
from jax.sharding import PartitionSpec as P

HEAD_P = 64
STATE = 128
SPAN = 64
HEAD_DIM = 128
BLOCK = 128


HIGHEST = lax.Precision.HIGHEST
NEGATIVE = -1e30


def passed_along(block, axis, distance):
    devices = range(lax.axis_size(axis))
    route = [(i - distance, i) for i in devices if i - distance in devices]
    return lax.ppermute(block, axis, route)


def span_pass(carried, pieces):
    inputs, in_narrow, out_narrow, step_sizes, decays = pieces
    in_wide = in_narrow.astype(jnp.float32)
    out_wide = out_narrow.astype(jnp.float32)
    running = jnp.cumsum(decays, axis=1)
    length = decays.shape[1]
    row_index = lax.broadcasted_iota(jnp.int32, (length, length), 0)
    col_index = lax.broadcasted_iota(jnp.int32, (length, length), 1)
    causal = (row_index >= col_index)[None]
    spread_log = running[:, :, None] - running[:, None, :]
    retain = jnp.where(causal, jnp.exp(jnp.where(causal, spread_log, 0.0)), 0.0)
    intersection = jnp.dot(out_narrow, in_narrow.T, preferred_element_type=jnp.float32)
    weights = intersection[None] * retain * step_sizes[:, None, :]
    y_intra = jnp.einsum("hij,jhp->ihp", weights, inputs, precision=HIGHEST)
    y_inter = (
        jnp.einsum("in,hpn->ihp", out_wide, carried, precision=HIGHEST)
        * jnp.exp(running).T[:, :, None]
    )
    to_end = jnp.exp(running[:, -1:] - running) * step_sizes
    injected = jnp.einsum("hj,jhp,jn->hpn", to_end, inputs, in_wide, precision=HIGHEST)
    carried = jnp.exp(running[:, -1])[:, None, None] * carried + injected
    return (carried, y_intra + y_inter)


def attend(carry_now, query_portion, q_pos, q_table, k_piece, v_piece, k_start):
    row_top, row_total, accumulated = carry_now
    key_count = k_piece.shape[0]
    kv_local = query_portion.shape[0]
    head_dim = query_portion.shape[3]
    k_pos = k_start + jnp.arange(key_count, dtype=jnp.int32)
    k_block = k_pos // BLOCK
    k_onehot = (k_block[:, None] == jnp.arange(q_table.shape[1], dtype=jnp.int32)[None, :]).astype(
        jnp.float32
    )
    visible = (
        jnp.dot(q_table, k_onehot.T, precision=HIGHEST, preferred_element_type=jnp.float32) > 0.5
    )
    same_block = (q_pos // BLOCK)[:, None] == k_block[None, :]
    allowed = (k_pos[None, :] <= q_pos[:, None]) & (visible | same_block)
    key_grouped_rows = k_piece.reshape(key_count, kv_local, head_dim)
    v_grouped = v_piece.reshape(key_count, kv_local, head_dim)
    scores = jnp.einsum(
        "mohz,pmz->mohp", query_portion, key_grouped_rows, preferred_element_type=jnp.float32
    ) * head_dim ** (-0.5)
    scores = jnp.where(allowed[None, None], scores, NEGATIVE)
    new_top = jnp.maximum(row_top, jnp.max(scores, axis=-1))
    expo_terms = jnp.where(allowed[None, None], jnp.exp(scores - new_top[..., None]), 0.0)
    fading = jnp.exp(row_top - new_top)
    row_total = row_total * fading + jnp.sum(expo_terms, axis=-1)
    accumulated = accumulated * fading[..., None] + jnp.einsum(
        "abvu,uac->abvc",
        expo_terms.astype(jnp.bfloat16),
        v_grouped,
        preferred_element_type=jnp.float32,
    )
    return (new_top, row_total, accumulated)


def on_device(
    ssm_input,
    input_map,
    output_map,
    step_size,
    log_decay,
    skip_gain,
    norm_gain,
    query_weight,
    key_states,
    value_states,
    block_mask,
):
    length = ssm_input.shape[0]
    head_count = skip_gain.shape[0]
    span_count = length // SPAN
    inputs = ssm_input.astype(jnp.float32).reshape(length, head_count, HEAD_P)
    out_map = output_map.astype(jnp.float32)
    pieces = (
        inputs.reshape(span_count, SPAN, head_count, HEAD_P),
        input_map.reshape(span_count, SPAN, STATE),
        output_map.reshape(span_count, SPAN, STATE),
        step_size.reshape(head_count, span_count, SPAN).transpose(1, 0, 2),
        log_decay.reshape(head_count, span_count, SPAN).transpose(1, 0, 2),
    )
    local_state, outputs = lax.scan(
        span_pass, jnp.zeros((head_count, HEAD_P, STATE), jnp.float32), pieces
    )
    running = jnp.cumsum(log_decay, axis=1)
    through = running[:, -1]

    def relay(turn_index, arrived):
        outgoing = jnp.exp(through)[:, None, None] * arrived + local_state
        return passed_along(outgoing, "context", 1)

    incoming = lax.fori_loop(0, lax.axis_size("context") - 1, relay, jnp.zeros_like(local_state))
    carried_in = (
        jnp.einsum("tn,hpn->thp", out_map, incoming, precision=HIGHEST)
        * jnp.exp(running).T[:, :, None]
    )
    scan_out = (
        outputs.reshape(length, head_count, HEAD_P) + carried_in + skip_gain[None, :, None] * inputs
    )
    squares = jnp.mean(scan_out * scan_out, axis=-1, keepdims=True)
    normed = scan_out * lax.rsqrt(squares + 1e-05) * norm_gain.reshape(head_count, HEAD_P)
    mixer_out = normed.reshape(length, head_count * HEAD_P).astype(jnp.bfloat16)
    tensor_size = lax.axis_size("tensor")
    local_heads = query_weight.shape[1] // HEAD_DIM // tensor_size
    product = jnp.dot(mixer_out, query_weight, preferred_element_type=jnp.float32)
    query = lax.psum_scatter(
        product.reshape(length, local_heads * lax.axis_size("tensor"), HEAD_DIM).transpose(1, 0, 2),
        "tensor",
        scatter_dimension=0,
        tiled=True,
    ).astype(jnp.bfloat16)
    kv_local = key_states.shape[1] // HEAD_DIM
    group_size = local_heads // kv_local
    device_rank = lax.axis_index("context")
    row_order = jnp.arange(length, dtype=jnp.int32)
    q_at = device_rank * length + row_order
    set_count = 1
    grouped = query.reshape(kv_local, group_size, length, HEAD_DIM)
    block_count = block_mask.shape[0]
    q_onehot = (
        (q_at // BLOCK)[:, None] == jnp.arange(block_count, dtype=jnp.int32)[None, :]
    ).astype(jnp.float32)
    mask_table = jnp.dot(
        q_onehot,
        block_mask.astype(jnp.float32),
        precision=HIGHEST,
        preferred_element_type=jnp.float32,
    )
    set_rows = length // set_count
    q_sets = [grouped]
    pos_sets = [q_at]
    table_sets = [mask_table]
    last_sets = [jnp.max(position_part) for position_part in pos_sets]
    initial = tuple(
        (
            (
                jnp.full((kv_local, group_size, set_rows), NEGATIVE, jnp.float32),
                jnp.zeros((kv_local, group_size, set_rows), jnp.float32),
                jnp.zeros((kv_local, group_size, set_rows, HEAD_DIM), jnp.float32),
            )
            for member in range(set_count)
        )
    )
    k_all = lax.all_gather(key_states, "context", axis=0, tiled=True)
    v_all = lax.all_gather(value_states, "context", axis=0, tiled=True)
    key_count = k_all.shape[0]
    block_rows = math.gcd(key_count, 512)
    block_total = key_count // block_rows
    k_blocks = k_all.reshape(block_total, block_rows, k_all.shape[1])
    v_blocks = v_all.reshape(block_total, block_rows, v_all.shape[1])
    offsets = block_rows * jnp.arange(block_total, dtype=jnp.int32)

    def step_block(carry_list, block_parts):
        k_piece, v_piece, k_start = block_parts
        member = 0

        def compute(carry_now, member=member):
            return attend(
                carry_now,
                q_sets[member],
                pos_sets[member],
                table_sets[member],
                k_piece,
                v_piece,
                k_start,
            )

        def unchanged(carry_now):
            return carry_now

        updated = [lax.cond(k_start <= last_sets[member], compute, unchanged, carry_list[member])]
        return (tuple(updated), None)

    result_sets, ignored = lax.scan(step_block, initial, (k_blocks, v_blocks, offsets))
    finished = jnp.concatenate(
        [member_set[2] / member_set[1][..., None] for member_set in result_sets], axis=2
    )
    finished = finished.reshape(local_heads, length, HEAD_DIM).astype(jnp.bfloat16)
    attended = finished.transpose(1, 0, 2).reshape(length, local_heads * HEAD_DIM)
    return (mixer_out, attended)


def solution(mesh):
    return jax.shard_map(
        on_device,
        mesh=mesh,
        in_specs=(
            P(("dp", "context"), "tensor"),
            P(("dp", "context"), None),
            P(("dp", "context"), None),
            P("tensor", ("dp", "context")),
            P("tensor", ("dp", "context")),
            P("tensor"),
            P("tensor"),
            P("tensor", None),
            P(("dp", "context"), "tensor"),
            P(("dp", "context"), "tensor"),
            P("dp", None),
        ),
        out_specs=(P(("dp", "context"), "tensor"), P(("dp", "context"), "tensor")),
        check_vma=False,
    )
```

profile of v0, /device:TPU:26, one launch (start us, length us, event | category | flops | bytes accessed | tf_op | source)
XLA Modules:
  0.0 335.2 jit_solution(6111685917004146096)
XLA Ops:
  12.2 4.5 %reshape_reshape.3 = f32[4,64,32,64]{3,2,1,0:T(8,128)} reshape(bf16[256,2048]{1,0:T(8,128)(2,1)} %param.19) | data formatting | bytes 3145728 | tf_op jit(solution)/shard_map/reshape;reshape | solution.py:102
  18.5 143.1 %while.42 = (s32[]{:T(128)}, f32[32,64,128]{2,1,0:T(8,128)S(1)}, f32[4,64,32,64]{1,0,3,2:T(4,128)}, f32[4,32,64]{2,0,1:T(4,128)S(1)}, f32[4,32,64]{2,0,1:T(4,128...) while((s32[]{:T(128)}, f32[32,64,128]{2,1,0:T(8,128)S(1)}, ...), condition=%wide.region_2.3_spmd.clone, body=%wide.region_0.2_spmd.clone.sunk | while | flops 506599424 | bytes 9677072 | solution.py:108
  20.8 3.0 convolution_bitcast_fusion.3
  24.1 1.9 fusion.85
  26.0 27.0 %dynamic_update_slice.6 = f32[4,64,32,64]{1,0,3,2:T(4,128)} dynamic-update-slice(f32[4,64,32,64]{1,0,3,2:T(4,128)} %get-tuple-element.579, f32[1,64,32,64]{1,0,3,2:T(1,128)S(1)} %bitcast.152, s32[]{:T(128)} %get-tuple-element.577, s32[]{:T(128)} %constant.126.clone.1..sunk, s32[]{:T(128)} %constant.126.clone.1..sunk, s32[]{:T(128)} %constant.126.clone.1..sunk) | dynamic-update-slice | bytes 1048580 | tf_op jit(solution)/shard_map/while/body/jit(dynamic_update_index_in_dim)/dynamic_update_slice | solution.py:108
  56.6 3.0 convolution_bitcast_fusion.3
  59.9 1.9 fusion.85
  61.8 27.0 %dynamic_update_slice.6 = f32[4,64,32,64]{1,0,3,2:T(4,128)} dynamic-update-slice(f32[4,64,32,64]{1,0,3,2:T(4,128)} %get-tuple-element.579, f32[1,64,32,64]{1,0,3,2:T(1,128)S(1)} %bitcast.152, s32[]{:T(128)} %get-tuple-element.577, s32[]{:T(128)} %constant.126.clone.1..sunk, s32[]{:T(128)} %constant.126.clone.1..sunk, s32[]{:T(128)} %constant.126.clone.1..sunk) | dynamic-update-slice | bytes 1048580 | tf_op jit(solution)/shard_map/while/body/jit(dynamic_update_index_in_dim)/dynamic_update_slice | solution.py:108
  92.4 3.0 convolution_bitcast_fusion.3
  95.7 1.9 fusion.85
  97.6 27.0 %dynamic_update_slice.6 = f32[4,64,32,64]{1,0,3,2:T(4,128)} dynamic-update-slice(f32[4,64,32,64]{1,0,3,2:T(4,128)} %get-tuple-element.579, f32[1,64,32,64]{1,0,3,2:T(1,128)S(1)} %bitcast.152, s32[]{:T(128)} %get-tuple-element.577, s32[]{:T(128)} %constant.126.clone.1..sunk, s32[]{:T(128)} %constant.126.clone.1..sunk, s32[]{:T(128)} %constant.126.clone.1..sunk) | dynamic-update-slice | bytes 1048580 | tf_op jit(solution)/shard_map/while/body/jit(dynamic_update_index_in_dim)/dynamic_update_slice | solution.py:108
  128.2 3.0 convolution_bitcast_fusion.3
  131.5 1.9 fusion.85
  133.3 27.0 %dynamic_update_slice.6 = f32[4,64,32,64]{1,0,3,2:T(4,128)} dynamic-update-slice(f32[4,64,32,64]{1,0,3,2:T(4,128)} %get-tuple-element.579, f32[1,64,32,64]{1,0,3,2:T(1,128)S(1)} %bitcast.152, s32[]{:T(128)} %get-tuple-element.577, s32[]{:T(128)} %constant.126.clone.1..sunk, s32[]{:T(128)} %constant.126.clone.1..sunk, s32[]{:T(128)} %constant.126.clone.1..sunk) | dynamic-update-slice | bytes 1048580 | tf_op jit(solution)/shard_map/while/body/jit(dynamic_update_index_in_dim)/dynamic_update_slice | solution.py:108
  161.8 5.3 %reshape.177 = f32[256,32,64]{0,2,1:T(8,128)} reshape(f32[4,64,32,64]{1,0,3,2:T(4,128)} %get-tuple-element.243) | data formatting | bytes 4194304 | tf_op jit(solution)/shard_map/reshape | solution.py:124
  167.2 78.3 %while.40 = (s32[]{:T(128)}, f32[32,64,128]{2,1,0:T(8,128)S(1)}, f32[32,1,1]{0,2,1:T(1,128)S(1)}, f32[32,64,128]{2,1,0:T(8,128)S(1)}, s32[]{:T(128)}) while((s32[]{:T(128)}, f32[32,64,128]{2,1,0:T(8,128)S(1)}, f32[32,1,1]{0,2,1:T(1,128)S(1)}, f32[32,64,128]{2,1,0:T(8,128)S(1)}, s32[]{:T(128)}) %tuple.125), condition=%wide.region_6.7_spmd, body=%wide.region_5.6_spmd.sunk | while | flops 524290 | bytes 7340261 | solution.py:118
  168.7 25.5 %collective-permute-done = f32[32,64,128]{2,1,0:T(8,128)S(1)} collective-permute-done((f32[32,64,128]{2,1,0:T(8,128)S(1)}, f32[32,64,128]{2,1,0:T(8,128)S(1)}, u32[]{:S(2)}, u32[]{:S(2)}) %collective-permute-start) | collective-permute-done | bytes 1048608 | tf_op jit(solution)/shard_map/while/body/eval_jaxpr/ppermute | solution.py:22
  195.6 24.6 %collective-permute-done = f32[32,64,128]{2,1,0:T(8,128)S(1)} collective-permute-done((f32[32,64,128]{2,1,0:T(8,128)S(1)}, f32[32,64,128]{2,1,0:T(8,128)S(1)}, u32[]{:S(2)}, u32[]{:S(2)}) %collective-permute-start) | collective-permute-done | bytes 1048608 | tf_op jit(solution)/shard_map/while/body/eval_jaxpr/ppermute | solution.py:22
  221.7 23.7 %collective-permute-done = f32[32,64,128]{2,1,0:T(8,128)S(1)} collective-permute-done((f32[32,64,128]{2,1,0:T(8,128)S(1)}, f32[32,64,128]{2,1,0:T(8,128)S(1)}, u32[]{:S(2)}, u32[]{:S(2)}) %collective-permute-start) | collective-permute-done | bytes 1048608 | tf_op jit(solution)/shard_map/while/body/eval_jaxpr/ppermute | solution.py:22
  245.5 4.7 %multiply_reduce_fusion = (f32[256,32]{0,1:T(8,128)S(1)}, f32[256,32,64]{0,2,1:T(8,128)}) fusion(f32[256,32,64]{0,2,1:T(8,128)} %bitcast.158, f32[32]{0:T(128)S(1)} %copy-done.7, f32[256,32,64]{0,2,1:T(8,128)} %reshape.177, f32[256,32]{0,1:T(8,128)S(1)} %exponential_bitcast_fusion.1, f32[32,64,128]{2,1,0:T(8,128)S(1)} %get-tuple-element.245, ...), kind=kOutput, calls=%fused_computation.86 | convolution fusion | flops 808443904 | bytes 7471232 | tf_op jit(solution)/shard_map/tn,hpn->thp/dot_general | solution.py:120
  250.3 1.9 multiply_convert_fusion
  252.2 22.6 %copy.65 = bf16[4096,2048]{1,0:T(8,128)(2,1)} copy(bf16[4096,2048]{0,1:T(8,128)(2,1)} %bitcast.155) | data formatting | bytes 33554432 | tf_op jit(solution)/shard_map/dot_general | solution.py:131
  274.8 9.5 %convolution_bitcast_fusion.1 = f32[32,256,128]{2,1,0:T(8,128)} fusion(bf16[256,2048,1]{0,1,2:T(8,128)(2,1)S(1)} %bitcast.160, bf16[32,128,2048]{2,1,0:T(8,128)(2,1)} %bitcast.156), kind=kOutput, calls=%fused_computation.80 | convolution fusion | flops 4294967296 | bytes 22020096 | tf_op jit(solution)/shard_map/dot_general | solution.py:131
  289.7 8.1 %reduce-scatter.2.cloned.1.call-done = f32[16,256,128]{2,1,0:T(8,128)} async-done(((f32[32,256,128]{2,1,0:T(8,128)}), f32[16,256,128]{2,1,0:T(8,128)}) %reduce-scatter.2.cloned.1.call-update) | async-done | bytes 2097168 | tf_op jit(solution)/shard_map/reduce_scatter | solution.py:132
  301.1 22.8 %while.41 = (s32[]{:T(128)}, f32[4,4,256]{2,1,0:T(4,128)S(1)}, f32[4,4,256]{2,1,0:T(4,128)S(1)}, f32[4,4,256,128]{3,2,1,0:T(8,128)}, s32[2]{0:T(128)S(1)}, /*ind...) while((s32[]{:T(128)}, f32[4,4,256]{2,1,0:T(4,128)S(1)}, ...), condition=%wide.region_15.16_spmd.clone, body=%wide.region_10.15_spmd.clone.sunk | while | flops 1115316224 | bytes 51140960 | solution.py:200
  302.8 9.7 %conditional.3 = ((f32[4,4,256]{2,1,0:T(4,128)S(1)}, f32[4,4,256]{2,1,0:T(4,128)S(1)}, f32[4,4,256,128]{3,2,1,0:T(8,128)})) conditional(s32[]{:T(128)} %convert_element_type.52, (f32[4,4,256]{2,1,0:T(4,128)S(1)}, f32[4,4,256]{2,1,0:T(4,128)S(1)}, f32[4,4,256,128]{3,2,1,0:T(8,128)}) %tuple.94, (s32[]{:T(128)}, s32[]{:T(128)}, ...), branch_computations={%region_11.11_spmd, %region_12.14_spmd} | conditional | flops 1115316224 | bytes 51139684 | solution.py:197
  305.5 2.0 fusion.4
  307.6 3.5 %multiply_add_fusion.1 = f32[4,4,256,128]{3,2,1,0:T(8,128)S(1)} fusion(f32[4,4,256,128]{3,2,1,0:T(8,128)S(1)} %copy-done, bf16[512,4,128,1]{0,2,3,1:T(8,128)(2,1)S(1)} %bitcast.157, f32[4,512,4,256]{3,1,2,0:T(8,128)S(1)} %get-tuple-element.394, f32[4,4,256]{2,1,0:T(4,128)S(1)} %max.4, pred[256,512]{0,1:T(8,128)(4,1)S(1)} %fusion.12, ...), kind=kOutput, calls=%fused_computation.9 | convolution fusion | flops 548405248 | bytes 13271040 | tf_op jit(solution)/shard_map/while/body/eval_jaxpr/cond/branch_1_fun/abvu,uac->abvc/dot_general | solution.py:74
  314.2 9.7 %conditional.3 = ((f32[4,4,256]{2,1,0:T(4,128)S(1)}, f32[4,4,256]{2,1,0:T(4,128)S(1)}, f32[4,4,256,128]{3,2,1,0:T(8,128)})) conditional(s32[]{:T(128)} %convert_element_type.52, (f32[4,4,256]{2,1,0:T(4,128)S(1)}, f32[4,4,256]{2,1,0:T(4,128)S(1)}, f32[4,4,256,128]{3,2,1,0:T(8,128)}) %tuple.94, (s32[]{:T(128)}, s32[]{:T(128)}, ...), branch_computations={%region_11.11_spmd, %region_12.14_spmd} | conditional | flops 1115316224 | bytes 51139684 | solution.py:197
  316.9 2.0 fusion.4
  319.0 3.5 %multiply_add_fusion.1 = f32[4,4,256,128]{3,2,1,0:T(8,128)S(1)} fusion(f32[4,4,256,128]{3,2,1,0:T(8,128)S(1)} %copy-done, bf16[512,4,128,1]{0,2,3,1:T(8,128)(2,1)S(1)} %bitcast.157, f32[4,512,4,256]{3,1,2,0:T(8,128)S(1)} %get-tuple-element.394, f32[4,4,256]{2,1,0:T(4,128)S(1)} %max.4, pred[256,512]{0,1:T(8,128)(4,1)S(1)} %fusion.12, ...), kind=kOutput, calls=%fused_computation.9 | convolution fusion | flops 548405248 | bytes 13271040 | tf_op jit(solution)/shard_map/while/body/eval_jaxpr/cond/branch_1_fun/abvu,uac->abvc/dot_general | solution.py:74
  323.8 1.9 divide_convert_fusion
  (124 shorter events, 45.6 us)
Async XLA Ops:
  8.0 8.7 %copy-start.2 = (bf16[256,2048]{1,0:T(8,128)(2,1)S(1)}, bf16[256,2048]{1,0:T(8,128)(2,1)}, u32[]{:S(2)}) copy-start(bf16[256,2048]{1,0:T(8,128)(2,1)} %param.19) | copy-start | bytes 3145732
  8.0 278.6 %all-gather.3.cloned.1.call-start = ((), (), s32[]{:S(2)}) async-start(), calls=%async_computation.1 | async-start | bytes 1310720 | tf_op jit(solution)/shard_map/all_gather | solution.py:170
  8.7 279.4 %all-gather.5.cloned.1.call-start = ((), (), s32[]{:S(2)}) async-start(), calls=%async_computation.3 | async-start | bytes 1310720 | tf_op jit(solution)/shard_map/all_gather | solution.py:171
  9.5 288.2 %reduce-scatter.2.cloned.1.call-start = ((), (), s32[]{:S(2)}) async-start(), calls=%async_computation.2 | async-start | bytes 6291456 | tf_op jit(solution)/shard_map/reduce_scatter | solution.py:132
  12.1 6.2 %copy-start.5 = (f32[32,256]{1,0:T(8,128)S(1)}, f32[32,256]{1,0:T(8,128)}, u32[]{:S(2)}) copy-start(f32[32,256]{1,0:T(8,128)} %param.22) | copy-start | bytes 98308
  12.1 6.3 %copy-start.3 = (bf16[256,128]{1,0:T(8,128)(2,1)S(1)}, bf16[256,128]{1,0:T(8,128)(2,1)}, u32[]{:S(2)}) copy-start(bf16[256,128]{1,0:T(8,128)(2,1)} %param.21) | copy-start | bytes 196612
  12.2 6.3 %copy-start.4 = (bf16[256,128]{1,0:T(8,128)(2,1)S(1)}, bf16[256,128]{1,0:T(8,128)(2,1)}, u32[]{:S(2)}) copy-start(bf16[256,128]{1,0:T(8,128)(2,1)} %param.20) | copy-start | bytes 196612
  167.2 78.3 %copy-start.7 = (f32[32]{0:T(128)S(1)}, f32[32]{0:T(128)}, u32[]{:S(2)}) copy-start(f32[32]{0:T(128)} %param.24) | copy-start | bytes 388
  167.4 26.8 %collective-permute-start = (f32[32,64,128]{2,1,0:T(8,128)S(1)}, f32[32,64,128]{2,1,0:T(8,128)S(1)}, u32[]{:S(2)}, u32[]{:S(2)}) collective-permute-start(f32[32,64,128]{2,1,0:T(8,128)S(1)} %multiply_add_fusion.4), channel_id=1, source_target_pairs={{0,8},{8,16},{16,24},{1,9},{9,17},{17,25},{2,10},{10,18},{18,26},{... | collective-permute-start | bytes 3145736 | tf_op jit(solution)/shard_map/while/body/eval_jaxpr/ppermute | solution.py:22
  194.3 25.9 %collective-permute-start = (f32[32,64,128]{2,1,0:T(8,128)S(1)}, f32[32,64,128]{2,1,0:T(8,128)S(1)}, u32[]{:S(2)}, u32[]{:S(2)}) collective-permute-start(f32[32,64,128]{2,1,0:T(8,128)S(1)} %multiply_add_fusion.4), channel_id=1, source_target_pairs={{0,8},{8,16},{16,24},{1,9},{9,17},{17,25},{2,10},{10,18},{18,26},{... | collective-permute-start | bytes 3145736 | tf_op jit(solution)/shard_map/while/body/eval_jaxpr/ppermute | solution.py:22
  220.4 25.0 %collective-permute-start = (f32[32,64,128]{2,1,0:T(8,128)S(1)}, f32[32,64,128]{2,1,0:T(8,128)S(1)}, u32[]{:S(2)}, u32[]{:S(2)}) collective-permute-start(f32[32,64,128]{2,1,0:T(8,128)S(1)} %multiply_add_fusion.4), channel_id=1, source_target_pairs={{0,8},{8,16},{16,24},{1,9},{9,17},{17,25},{2,10},{10,18},{18,26},{... | collective-permute-start | bytes 3145736 | tf_op jit(solution)/shard_map/while/body/eval_jaxpr/ppermute | solution.py:22
  245.4 4.7 %copy-start.6 = (f32[2048]{0:T(1024)S(1)}, f32[2048]{0:T(1024)}, u32[]{:S(2)}) copy-start(f32[2048]{0:T(1024)} %param.25) | copy-start | bytes 24580
  284.3 2.1 copy-start.8
  305.5 2.1 copy-start
  311.1 1.3 copy-start.1
  316.9 2.1 copy-start
  322.5 1.3 copy-start.1
Sparse Core Ops, SparseCore 0:
  10.4 27.4 all-gather.2
  39.6 27.4 all-gather.4
Sparse Core Ops, SparseCore 1:
  284.4 13.3 reduce-scatter.1
where the time goes:
time: 340 us; the launch traced here: 335 us
  local copies, waits for them, and re-layouts  165 us (49%)
  waiting for transfers between devices  83.3 us (24%)
  matrix products  50.5 us (15%)
  between operations  15.7 us (5%)
  other arithmetic  14 us (4%)
  starting transfers between devices  3.99 us (1%)
    dynamic_update_slice x4, local copies, waits for them, and re-layouts, on_device(): lax.scan(span_pass, jnp.zeros((head_count, HEAD_P, STATE), jnp.float32),...  108 us
    ppermute x3, waiting for transfers between devices, passed_along(): return lax.ppermute(block, axis, route)  73.8 us
    dot_general x1, local copies, waits for them, and re-layouts, on_device(): jnp.dot(mixer_out, query_weight, preferred_element_type=jnp.float32)  22.6 us
    dot_general x4, matrix products, span_pass(): y_intra = jnp.einsum('hij,jhp->ihp', weights, inputs, precision=HIGHEST)  12.2 us
    dot_general x1, matrix products, on_device(): jnp.dot(mixer_out, query_weight, preferred_element_type=jnp.float32)  9.47 us
    reduce_scatter x1, waiting for transfers between devices, on_device(): lax.psum_scatter(product.reshape(length, local_heads * lax.axis_size('ten...  8.07 us
    dynamic_slice x12, local copies, waits for them, and re-layouts, on_device(): lax.scan(span_pass, jnp.zeros((head_count, HEAD_P, STATE), jnp.float32),...  7.87 us
    dot_general x4, matrix products, span_pass(): jnp.einsum('in,hpn->ihp', out_wide, carried, precision=HIGHEST)  7.48 us
  transfers between devices with their start and end apart: 6, of which 4 were waited for; matrix products, arithmetic and copies ran while one was open for 60% of the time, Pallas kernels for 0%

commit v1 on v0

v1 whole, which is shorter than its diff:
```python
import functools

import jax
import jax.numpy as jnp
from jax import lax
from jax.experimental import pallas as pl
from jax.experimental.pallas import tpu as pltpu
from jax.sharding import PartitionSpec as P

HEAD_P = 64
STATE = 128
HEAD_DIM = 128
BLOCK = 128
CHUNK = 256
NEGATIVE = -1e30
LOG2E = 1.4426950408889634
HIGHEST = lax.Precision.HIGHEST
MESH = pl.DeviceIdType.MESH
F32 = jnp.float32
BF16 = jnp.bfloat16
NT = (((1,), (1,)), ((), ()))


def split(wide):
    high = wide.astype(BF16)
    return high, (wide - high.astype(F32)).astype(BF16)


def dot(a, b):
    return jnp.dot(a, b, preferred_element_type=F32)


def kernel(
    n,
    mask_ref,
    x_ref,
    b_ref,
    c_ref,
    dt_ref,
    ld_ref,
    skip_ref,
    gain_ref,
    w_ref,
    k_ref,
    v_ref,
    mixer_ref,
    attended_ref,
    kv,
    w_own,
    w_other,
    bt,
    gram,
    col_run,
    col_dt,
    row_run,
    row_dt,
    state,
    arrived,
    mixed,
    mixed_other,
    q_acc,
    q_all,
    bias,
    top,
    total,
    acc,
    kv_send,
    kv_recv,
    st_send,
    st_recv,
    mx_send,
    mx_recv,
    wt_send,
    wt_recv,
    wt_own,
):
    me = lax.axis_index("context")
    core = lax.axis_index("tensor")
    other = 1 - core
    length = x_ref.shape[0]
    chunks = x_ref.shape[1] // CHUNK
    q_cols = w_own.shape[2]
    has_left = me > 0
    has_right = me < n - 1
    heads = q_cols // HEAD_DIM
    group = heads // (k_ref.shape[1] // HEAD_DIM)
    blocks = length // BLOCK

    barrier = pltpu.get_barrier_semaphore()
    pl.semaphore_signal(barrier, inc=1, device_id={"tensor": other}, device_id_type=MESH)

    @pl.when(has_left)
    def _():
        pl.semaphore_signal(barrier, inc=1, device_id={"context": me - 1}, device_id_type=MESH)

    @pl.when(has_right)
    def _():
        pl.semaphore_signal(barrier, inc=1, device_id={"context": me + 1}, device_id_type=MESH)

    peers = 1 + has_left.astype(jnp.int32) + has_right.astype(jnp.int32)
    pl.semaphore_wait(barrier, peers)

    def kv_copy(slot):
        return pltpu.make_async_remote_copy(
            src_ref=kv.at[slot],
            dst_ref=kv.at[slot + 1],
            send_sem=kv_send.at[slot],
            recv_sem=kv_recv.at[slot + 1],
            device_id={"context": me + 1},
            device_id_type=MESH,
        )

    def kv_wait(slot):
        pltpu.make_async_remote_copy(
            src_ref=kv.at[slot - 1],
            dst_ref=kv.at[slot],
            send_sem=kv_send.at[slot - 1],
            recv_sem=kv_recv.at[slot],
            device_id={"context": me - 1},
            device_id_type=MESH,
        ).wait_recv()

    def state_copy(j):
        return pltpu.make_async_remote_copy(
            src_ref=state.at[j],
            dst_ref=arrived.at[j],
            send_sem=st_send.at[j],
            recv_sem=st_recv.at[j],
            device_id={"context": me + 1},
            device_id_type=MESH,
        )

    def mixed_copy(j):
        return pltpu.make_async_remote_copy(
            src_ref=mixed.at[j],
            dst_ref=mixed_other.at[j],
            send_sem=mx_send.at[j],
            recv_sem=mx_recv.at[j],
            device_id={"tensor": other},
            device_id_type=MESH,
        )

    def rows_of(j):
        return pl.ds(pl.multiple_of(j * CHUNK, CHUNK), CHUNK)

    def weight_out(j):
        return pltpu.make_async_remote_copy(
            src_ref=w_ref.at[rows_of(j), pl.ds(pl.multiple_of(other * q_cols, CHUNK), q_cols)],
            dst_ref=w_other.at[j],
            send_sem=wt_send.at[j],
            recv_sem=wt_recv.at[j],
            device_id={"tensor": other},
            device_id_type=MESH,
        )

    def weight_in(j):
        return pltpu.make_async_copy(
            w_ref.at[rows_of(j), pl.ds(pl.multiple_of(core * q_cols, CHUNK), q_cols)],
            w_own.at[j],
            wt_own.at[j],
        )

    kv[0, 0] = k_ref[...]
    kv[0, 1] = v_ref[...]

    @pl.when(has_right)
    def _():
        kv_copy(0).start()

    @pl.loop(0, chunks)
    def _(j):
        weight_in(j).start()
        weight_out(j).start()

    row = lax.broadcasted_iota(jnp.int32, (length, length), 0)
    col = lax.broadcasted_iota(jnp.int32, (length, length), 1)
    causal = row >= col
    tri = jnp.where(causal, 1.0, 0.0).astype(F32)
    eye = jnp.where(row == col, 1.0, 0.0).astype(F32)
    run_rows = lax.dot_general(ld_ref[...], tri, NT, precision=HIGHEST, preferred_element_type=F32)
    run_cols = lax.dot_general(tri, ld_ref[...], NT, precision=HIGHEST, preferred_element_type=F32)
    dt_cols = lax.dot_general(eye, dt_ref[...], NT, precision=HIGHEST, preferred_element_type=F32)
    per = CHUNK // HEAD_P
    for j in range(chunks):
        col_run[j] = run_cols[:, j * per : (j + 1) * per]
        col_dt[j] = dt_cols[:, j * per : (j + 1) * per]
        row_run[j] = run_rows[j * per : (j + 1) * per, :]
        row_dt[j] = dt_ref[j * per : (j + 1) * per, :]
    bt[...] = jnp.transpose(b_ref[...].astype(F32)).astype(BF16)
    gram[...] = jnp.where(
        causal, lax.dot_general(c_ref[...], b_ref[...], NT, preferred_element_type=F32), 0.0
    )
    first = lax.broadcasted_iota(jnp.int32, (1, 128), 1) < HEAD_P

    @pl.when(me == 0)
    def _():
        arrived[...] = jnp.zeros_like(arrived)

    def lanes_of(j, pair):
        return pl.ds(pl.multiple_of(j * CHUNK + pair * 128, 128), 128)

    @pl.loop(0, chunks)
    def _(j):
        runs = col_run[j]
        steps = col_dt[j]
        for pair in range(CHUNK // 128):
            a = 2 * pair
            run = jnp.where(first, runs[:, a : a + 1], runs[:, a + 1 : a + 2])
            step = jnp.where(first, steps[:, a : a + 1], steps[:, a + 1 : a + 2])
            weighted = x_ref[:, lanes_of(j, pair)].astype(F32) * (
                jnp.exp(run[length - 1 : length, :] - run) * step
            )
            high, low = split(weighted)
            state[j, :, pair * 128 : (pair + 1) * 128] = dot(bt[...], high) + dot(bt[...], low)

        @pl.when(me == 0)
        def _():
            if n > 1:
                state_copy(j).start()

    q_acc[...] = jnp.zeros_like(q_acc)

    def add_query(part, weight):
        for t in range(0, q_cols, 512):
            q_acc[:, t : t + 512] += dot(part[...], weight[:, t : t + 512])

    def take_other(j):
        mixed_copy(j).wait_recv()
        weight_out(j).wait_recv()
        add_query(mixed_other.at[j], w_other.at[j])

    half = length // 2

    @pl.loop(0, chunks)
    def _(j):
        runs = col_run[j]

        @pl.when(has_left)
        def _():
            state_copy(j).wait_recv()

        @pl.when(has_left & has_right)
        def _():
            ends = runs[length - 1 : length, :]
            for pair in range(CHUNK // 128):
                a = 2 * pair
                keep = jnp.exp(jnp.where(first, ends[:, a : a + 1], ends[:, a + 1 : a + 2]))
                lanes = slice(pair * 128, (pair + 1) * 128)
                state[j, :, lanes] = keep * arrived[j, :, lanes] + state[j, :, lanes]
            state_copy(j).start()

        run_row = row_run[j]
        dt_row = row_dt[j]
        for pair in range(CHUNK // 128):
            lanes = lanes_of(j, pair)
            x_pair = x_ref[:, lanes]
            x_wide = x_pair.astype(F32)
            upper = jnp.zeros((half, 128), F32)
            lower = jnp.zeros((length - half, 128), F32)
            for member in range(2):
                a = 2 * pair + member
                x_own = jnp.where(first if member == 0 else ~first, x_wide, 0.0).astype(BF16)
                run_c = runs[:, a : a + 1]
                run_r = run_row[a : a + 1, :]
                dt_r = dt_row[a : a + 1, :]
                w_up = (
                    gram[:half, :half]
                    * jnp.exp(jnp.minimum(run_c[:half] - run_r[:, :half], 0.0))
                    * dt_r[:, :half]
                )
                high, low = split(w_up)
                upper = upper + dot(high, x_own[:half]) + dot(low, x_own[:half])
                w_low = gram[half:, :] * jnp.exp(jnp.minimum(run_c[half:] - run_r, 0.0)) * dt_r
                high, low = split(w_low)
                lower = lower + dot(high, x_own) + dot(low, x_own)
            high, low = split(arrived[j, :, pair * 128 : (pair + 1) * 128])
            carried = dot(c_ref[...], high) + dot(c_ref[...], low)
            a = 2 * pair
            grown = jnp.exp(jnp.where(first, runs[:, a : a + 1], runs[:, a + 1 : a + 2]))
            y = (
                jnp.concatenate([upper, lower], axis=0)
                + carried * grown
                + skip_ref[:, lanes] * x_wide
            )
            squares = y * y
            both = jnp.sum(squares, axis=1, keepdims=True)
            left = jnp.sum(jnp.where(first, squares, 0.0), axis=1, keepdims=True)
            right = jnp.sum(jnp.where(first, 0.0, squares), axis=1, keepdims=True)
            mean = jnp.where(first, left, right) * (1.0 / HEAD_P)
            out = (y * lax.rsqrt(mean + 1e-05) * gain_ref[:, lanes]).astype(BF16)
            mixed[j, :, pair * 128 : (pair + 1) * 128] = out
            mixer_ref[:, lanes] = out
        mixed_copy(j).start()
        weight_in(j).wait()
        add_query(mixed.at[j], w_own.at[j])

        @pl.when(j >= 1)
        def _():
            take_other(j - 1)

        @pl.when((j == 2) & has_left)
        def _():
            kv_wait(1)

        @pl.when((j == 2) & has_left & has_right)
        def _():
            kv_copy(1).start()

    take_other(chunks - 1)
    q_all[...] = q_acc[...].astype(BF16)
    top[...] = jnp.full_like(top, NEGATIVE)
    total[...] = jnp.zeros_like(total)
    acc[...] = jnp.zeros_like(acc)
    scale = HEAD_DIM ** (-0.5) * LOG2E

    def attend(slot):
        for i in range(blocks):
            for m in range(blocks):
                seen = mask_ref[me * blocks + i, (me - slot) * blocks + m] == 1
                bias[i * BLOCK : (i + 1) * BLOCK, m * BLOCK : (m + 1) * BLOCK] = jnp.full(
                    (BLOCK, BLOCK), jnp.where(seen, 0.0, NEGATIVE), F32
                )

        @pl.when(slot == 0)
        def _():
            same = (row // BLOCK) == (col // BLOCK)
            bias[...] = jnp.where(causal, jnp.where(same, 0.0, bias[...]), NEGATIVE)

        @pl.loop(0, heads)
        def _(h):
            mine = pl.ds(pl.multiple_of(h * HEAD_DIM, HEAD_DIM), HEAD_DIM)
            shared = pl.ds(pl.multiple_of((h // group) * HEAD_DIM, HEAD_DIM), HEAD_DIM)
            keys = kv[slot, 0, :, shared]
            values = kv[slot, 1, :, shared]
            scores = (
                lax.dot_general(q_all[:, mine], keys, NT, preferred_element_type=F32) + bias[...]
            )
            old_top = top[h]
            new_top = jnp.maximum(old_top, jnp.max(scores, axis=1, keepdims=True))
            fade = jnp.exp2((old_top - new_top) * scale)
            parts = [
                jnp.exp2((scores[:, t : t + 128] - new_top) * scale) for t in range(0, length, 128)
            ]
            summed = parts[0]
            for part in parts[1:]:
                summed = summed + part
            total[h] = total[h] * fade + summed
            weights = jnp.concatenate([part.astype(BF16) for part in parts], axis=1)
            acc[h] = acc[h] * fade + dot(weights, values)
            top[h] = new_top

    @pl.loop(0, n)
    def _(slot):
        @pl.when(slot <= me)
        def _():
            @pl.when(slot >= 2)
            def _():
                kv_wait(slot)

            @pl.when((slot >= 2) & has_right)
            def _():
                kv_copy(slot).start()

            attend(slot)

    @pl.loop(0, heads)
    def _(h):
        mine = pl.ds(pl.multiple_of(h * HEAD_DIM, HEAD_DIM), HEAD_DIM)
        attended_ref[:, mine] = (acc[h] / jnp.sum(total[h], axis=1, keepdims=True)).astype(BF16)

    @pl.loop(0, chunks)
    def _(j):
        mixed_copy(j).wait_send()
        weight_out(j).wait_send()

        @pl.when(has_right)
        def _():
            state_copy(j).wait_send()

    @pl.loop(0, n)
    def _(slot):
        @pl.when((slot <= me) & has_right)
        def _():
            kv_copy(slot).wait_send()


def on_device(
    ssm_input,
    input_map,
    output_map,
    step_size,
    log_decay,
    skip_gain,
    norm_gain,
    query_weight,
    key_states,
    value_states,
    block_mask,
):
    n = lax.axis_size("context")
    length, channels = ssm_input.shape
    q_cols = query_weight.shape[1] // lax.axis_size("tensor")
    chunks = channels // CHUNK
    heads = q_cols // HEAD_DIM
    per = CHUNK // HEAD_P
    kv_cols = key_states.shape[1]
    skip = jnp.repeat(skip_gain, HEAD_P).reshape(1, channels)
    vmem = pl.BlockSpec(memory_space=pltpu.VMEM)
    dma = pltpu.SemaphoreType.DMA
    out = jax.ShapeDtypeStruct((length, channels), BF16)
    return pl.pallas_call(
        functools.partial(kernel, n),
        out_shape=(out, jax.ShapeDtypeStruct((length, q_cols), BF16)),
        in_specs=[pl.BlockSpec(memory_space=pltpu.SMEM)]
        + [vmem] * 7
        + [pl.BlockSpec(memory_space=pl.ANY)]
        + [vmem] * 2,
        out_specs=(vmem, vmem),
        scratch_shapes=[
            pltpu.VMEM((n, 2, length, kv_cols), BF16),
            pltpu.VMEM((chunks, CHUNK, q_cols), BF16),
            pltpu.VMEM((chunks, CHUNK, q_cols), BF16),
            pltpu.VMEM((STATE, length), BF16),
            pltpu.VMEM((length, length), F32),
            pltpu.VMEM((chunks, length, per), F32),
            pltpu.VMEM((chunks, length, per), F32),
            pltpu.VMEM((chunks, per, length), F32),
            pltpu.VMEM((chunks, per, length), F32),
            pltpu.VMEM((chunks, STATE, CHUNK), F32),
            pltpu.VMEM((chunks, STATE, CHUNK), F32),
            pltpu.VMEM((chunks, length, CHUNK), BF16),
            pltpu.VMEM((chunks, length, CHUNK), BF16),
            pltpu.VMEM((length, q_cols), F32),
            pltpu.VMEM((length, q_cols), BF16),
            pltpu.VMEM((length, length), F32),
            pltpu.VMEM((heads, length, HEAD_DIM), F32),
            pltpu.VMEM((heads, length, HEAD_DIM), F32),
            pltpu.VMEM((heads, length, HEAD_DIM), F32),
            dma((n,)),
            dma((n + 1,)),
            dma((chunks,)),
            dma((chunks,)),
            dma((chunks,)),
            dma((chunks,)),
            dma((chunks,)),
            dma((chunks,)),
            dma((chunks,)),
        ],
        compiler_params=pltpu.CompilerParams(
            collective_id=0, has_side_effects=True, vmem_limit_bytes=56 * 1024 * 1024
        ),
        name="mixer_attention",
    )(
        block_mask,
        ssm_input,
        input_map,
        output_map,
        step_size,
        log_decay,
        skip,
        norm_gain.reshape(1, channels),
        query_weight,
        key_states,
        value_states,
    )


def solution(mesh):
    return jax.shard_map(
        on_device,
        mesh=mesh,
        in_specs=(
            P(("dp", "context"), "tensor"),
            P(("dp", "context"), None),
            P(("dp", "context"), None),
            P("tensor", ("dp", "context")),
            P("tensor", ("dp", "context")),
            P("tensor"),
            P("tensor"),
            P("tensor", None),
            P(("dp", "context"), "tensor"),
            P(("dp", "context"), "tensor"),
            P("dp", None),
        ),
        out_specs=(P(("dp", "context"), "tensor"), P(("dp", "context"), "tensor")),
        check_vma=False,
    )
```

time: 340 us -> 101 us (0.30); the launches traced: 335 us -> 100 us
  local copies, waits for them, and re-layouts: 165 us -> 6.01 us
  Pallas kernels: 0 us -> 93.8 us
  waiting for transfers between devices: 83.3 us -> 0 us
  matrix products: 50.5 us -> 0 us
  between operations: 15.7 us -> 0.64 us
  other arithmetic: 14 us -> 0 us
  starting transfers between devices: 3.99 us -> 0 us
    dynamic_update_slice x4 -> x0, local copies, waits for them, and re-layouts: 108 us -> none  [on_device(): lax.scan(span_pass, jnp.zeros((head_count, HEAD_P, STATE), jnp.float32),...]
    pallas_call x0 -> x1, Pallas kernels: none -> 93.8 us  [on_device(): pl.pallas_call(functools.partial(kernel, n), out_shape=(out, jax.ShapeDty...]
    ppermute x3 -> x0, waiting for transfers between devices: 73.8 us -> none  [passed_along(): return lax.ppermute(block, axis, route)]
    dot_general x25 -> x0, matrix products: 50.5 us -> none  [the longest x4 12.2 us: span_pass(): y_intra = jnp.einsum('hij,jhp->ihp', weights, inputs, precision=HIGHEST)]
    dot_general x1 -> x0, local copies, waits for them, and re-layouts: 22.6 us -> none  [on_device(): jnp.dot(mixer_out, query_weight, preferred_element_type=jnp.float32)]
    dynamic_slice x16 -> x0, local copies, waits for them, and re-layouts: 9.13 us -> none  [the longest x12 7.87 us: on_device(): lax.scan(span_pass, jnp.zeros((head_count, HEAD_P, STATE), jnp.float32),...]
    reduce_scatter x1 -> x0, waiting for transfers between devices: 8.07 us -> none  [on_device(): lax.psum_scatter(product.reshape(length, local_heads * lax.axis_size('ten...]
    reshape x4 -> x0, local copies, waits for them, and re-layouts: 7 us -> none  [the longest x1 5.3 us: on_device(): outputs.reshape(length, head_count, HEAD_P) + carried_in]
  transfers between devices with their start and end apart: 6 -> 0, of which waited for: 4 -> 0; matrix products, arithmetic and copies ran while one was open for 60% -> 0% of each run, Pallas kernels for 0% -> 0%
where the time goes in v1:
time: 101 us; the launch traced here: 100 us
  Pallas kernels  93.8 us (93%)
  local copies, waits for them, and re-layouts  6.01 us (6%)
    pallas_call x1, Pallas kernels, on_device(): pl.pallas_call(functools.partial(kernel, n), out_shape=(out, jax.ShapeDty...  93.8 us
    unnamed x2, local copies, waits for them, and re-layouts  4.61 us

profile of v1, /device:TPU:26, one launch (start us, length us, event | category | flops | bytes accessed | tf_op | source)
XLA Modules:
  0.0 100.4 jit_solution(1147487684626589084)
XLA Ops:
  0.6 0.7 broadcast_in_dim.3
  1.4 0.7 reshape_reshape.3.skip_ref
  2.0 93.8 %mixer_attention.1 = (bf16[256,2048]{1,0:T(8,128)(2,1)}, bf16[256,2048]{1,0:T(8,128)(2,1)}) custom-call(s32[8,8]{1,0:T(8,128)} %mask_ref.1, bf16[256,2048]{1,0:T(8,128)(2,1)} %x_ref.1, bf16[256,128]{1,0:T(8,128)(2,1)} %b_ref.1, bf16[256,128]{1,0:T(8,128)(2,1)} %c_ref.1, f32[32,256]{1,0:T(8,128)} %dt_ref.1, f32[32,256]{1,0:T(8,128)} %ld_ref.1, ...), custom_call_target="tpu_custom_call" | custom-call | tf_op jit(solution)/shard_map/mixer_attention/pallas_call | solution.py:411
  95.8 2.3 %copy.15 = bf16[256,2048]{1,0:T(8,128)(2,1)} copy(bf16[256,2048]{1,0:T(8,128)(2,1)} %get-tuple-element.4) | data formatting | bytes 2097152
  98.1 2.3 %copy.16 = bf16[256,2048]{1,0:T(8,128)(2,1)} copy(bf16[256,2048]{1,0:T(8,128)(2,1)} %get-tuple-element.5) | data formatting | bytes 2097152

commit v2 on v1

--- a/solution.py
+++ b/solution.py
@@ -23,11 +23,23 @@
 
 def split(wide):
     high = wide.astype(BF16)
-    return high, (wide - high.astype(F32)).astype(BF16)
+    rest = wide - high.astype(F32)
+    middle = rest.astype(BF16)
+    return high, middle, (rest - middle.astype(F32)).astype(BF16)
 
 
 def dot(a, b):
     return jnp.dot(a, b, preferred_element_type=F32)
+
+
+def dot_left(wide, narrow):
+    high, middle, low = split(wide)
+    return dot(high, narrow) + (dot(middle, narrow) + dot(low, narrow))
+
+
+def dot_right(narrow, wide):
+    high, middle, low = split(wide)
+    return dot(narrow, high) + (dot(narrow, middle) + dot(narrow, low))
 
 
 def kernel(
@@ -61,6 +73,7 @@
     q_acc,
     q_all,
     bias,
+    weights,
     top,
     total,
     acc,
@@ -100,25 +113,31 @@
     peers = 1 + has_left.astype(jnp.int32) + has_right.astype(jnp.int32)
     pl.semaphore_wait(barrier, peers)
 
-    def kv_copy(slot):
+    def pass_on(which, slot):
         return pltpu.make_async_remote_copy(
-            src_ref=kv.at[slot],
-            dst_ref=kv.at[slot + 1],
-            send_sem=kv_send.at[slot],
-            recv_sem=kv_recv.at[slot + 1],
+            src_ref=kv.at[which, slot],
+            dst_ref=kv.at[which, slot + 1],
+            send_sem=kv_send.at[which, slot],
+            recv_sem=kv_recv.at[which, slot + 1],
             device_id={"context": me + 1},
             device_id_type=MESH,
         )
 
-    def kv_wait(slot):
-        pltpu.make_async_remote_copy(
-            src_ref=kv.at[slot - 1],
-            dst_ref=kv.at[slot],
-            send_sem=kv_send.at[slot - 1],
-            recv_sem=kv_recv.at[slot],
-            device_id={"context": me - 1},
-            device_id_type=MESH,
-        ).wait_recv()
+    def take(which, slot):
+        @pl.when((slot >= 1) & (slot <= me))
+        def _():
+            pltpu.make_async_remote_copy(
+                src_ref=kv.at[which, slot - 1],
+                dst_ref=kv.at[which, slot],
+                send_sem=kv_send.at[which, slot - 1],
+                recv_sem=kv_recv.at[which, slot],
+                device_id={"context": me - 1},
+                device_id_type=MESH,
+            ).wait_recv()
+
+            @pl.when(has_right)
+            def _():
+                pass_on(which, slot).start()
 
     def state_copy(j):
         return pltpu.make_async_remote_copy(
@@ -161,11 +180,12 @@
         )
 
     kv[0, 0] = k_ref[...]
-    kv[0, 1] = v_ref[...]
-
-    @pl.when(has_right)
+    kv[1, 0] = v_ref[...]
+
+    @pl.when(has_left & has_right)
     def _():
-        kv_copy(0).start()
+        pass_on(0, 0).start()
+        pass_on(1, 0).start()
 
     @pl.loop(0, chunks)
     def _(j):
@@ -210,14 +230,33 @@
             weighted = x_ref[:, lanes_of(j, pair)].astype(F32) * (
                 jnp.exp(run[length - 1 : length, :] - run) * step
             )
-            high, low = split(weighted)
-            state[j, :, pair * 128 : (pair + 1) * 128] = dot(bt[...], high) + dot(bt[...], low)
+            state[j, :, pair * 128 : (pair + 1) * 128] = dot_right(bt[...], weighted)
 
         @pl.when(me == 0)
         def _():
             if n > 1:
                 state_copy(j).start()
 
+    @pl.when(me == 0)
+    def _():
+        if n > 1:
+            pass_on(0, 0).start()
+            pass_on(1, 0).start()
+
+    same = (row // BLOCK) == (col // BLOCK)
+
+    @pl.loop(0, n)
+    def _(slot):
+        @pl.when(slot <= me)
+        def _():
+            for i in range(blocks):
+                for m in range(blocks):
+                    seen = mask_ref[me * blocks + i, (me - slot) * blocks + m] == 1
+                    bias[slot, i * BLOCK : (i + 1) * BLOCK, m * BLOCK : (m + 1) * BLOCK] = jnp.full(
+                        (BLOCK, BLOCK), jnp.where(seen, 0.0, NEGATIVE), F32
+                    )
+
+    bias[0] = jnp.where(causal, jnp.where(same, 0.0, bias[0]), NEGATIVE)
     q_acc[...] = jnp.zeros_like(q_acc)
 
     def add_query(part, weight):
@@ -268,19 +307,16 @@
                     * jnp.exp(jnp.minimum(run_c[:half] - run_r[:, :half], 0.0))
                     * dt_r[:, :half]
                 )
-                high, low = split(w_up)
-                upper = upper + dot(high, x_own[:half]) + dot(low, x_own[:half])
+                upper = upper + dot_left(w_up, x_own[:half])
                 w_low = gram[half:, :] * jnp.exp(jnp.minimum(run_c[half:] - run_r, 0.0)) * dt_r
-                high, low = split(w_low)
-                lower = lower + dot(high, x_own) + dot(low, x_own)
-            high, low = split(arrived[j, :, pair * 128 : (pair + 1) * 128])
-            carried = dot(c_ref[...], high) + dot(c_ref[...], low)
+                lower = lower + dot_left(w_low, x_own)
+            carried = dot_right(c_ref[...], arrived[j, :, pair * 128 : (pair + 1) * 128])
             a = 2 * pair
             grown = jnp.exp(jnp.where(first, runs[:, a : a + 1], runs[:, a + 1 : a + 2]))
             y = (
                 jnp.concatenate([upper, lower], axis=0)
                 + carried * grown
-                + skip_ref[:, lanes] * x_wide
+                + jnp.where(first, skip_ref[j * per + a], skip_ref[j * per + a + 1]) * x_wide
             )
             squares = y * y
             both = jnp.sum(squares, axis=1, keepdims=True)
@@ -298,75 +334,88 @@
         def _():
             take_other(j - 1)
 
-        @pl.when((j == 2) & has_left)
-        def _():
-            kv_wait(1)
-
-        @pl.when((j == 2) & has_left & has_right)
-        def _():
-            kv_copy(1).start()
-
     take_other(chunks - 1)
+
+    @pl.when(has_right)
+    def _():
+        for which in range(2):
+
+            @pl.loop(1, n)
+            def _(slot, which=which):
+                take(which, slot)
+
     q_all[...] = q_acc[...].astype(BF16)
     top[...] = jnp.full_like(top, NEGATIVE)
     total[...] = jnp.zeros_like(total)
     acc[...] = jnp.zeros_like(acc)
     scale = HEAD_DIM ** (-0.5) * LOG2E
 
-    def attend(slot):
-        for i in range(blocks):
-            for m in range(blocks):
-                seen = mask_ref[me * blocks + i, (me - slot) * blocks + m] == 1
-                bias[i * BLOCK : (i + 1) * BLOCK, m * BLOCK : (m + 1) * BLOCK] = jnp.full(
-                    (BLOCK, BLOCK), jnp.where(seen, 0.0, NEGATIVE), F32
-                )
-
-        @pl.when(slot == 0)
-        def _():
-            same = (row // BLOCK) == (col // BLOCK)
-            bias[...] = jnp.where(causal, jnp.where(same, 0.0, bias[...]), NEGATIVE)
-
-        @pl.loop(0, heads)
-        def _(h):
-            mine = pl.ds(pl.multiple_of(h * HEAD_DIM, HEAD_DIM), HEAD_DIM)
-            shared = pl.ds(pl.multiple_of((h // group) * HEAD_DIM, HEAD_DIM), HEAD_DIM)
-            keys = kv[slot, 0, :, shared]
-            values = kv[slot, 1, :, shared]
-            scores = (
-                lax.dot_general(q_all[:, mine], keys, NT, preferred_element_type=F32) + bias[...]
-            )
-            old_top = top[h]
-            new_top = jnp.maximum(old_top, jnp.max(scores, axis=1, keepdims=True))
-            fade = jnp.exp2((old_top - new_top) * scale)
-            parts = [
-                jnp.exp2((scores[:, t : t + 128] - new_top) * scale) for t in range(0, length, 128)
-            ]
-            summed = parts[0]
-            for part in parts[1:]:
-                summed = summed + part
-            total[h] = total[h] * fade + summed
-            weights = jnp.concatenate([part.astype(BF16) for part in parts], axis=1)
-            acc[h] = acc[h] * fade + dot(weights, values)
-            top[h] = new_top
+    def head_lanes(h):
+        return pl.ds(pl.multiple_of(h * HEAD_DIM, HEAD_DIM), HEAD_DIM)
+
+    def scores_of(slot, h, keys):
+        return (
+            lax.dot_general(q_all[:, head_lanes(h)], keys, NT, preferred_element_type=F32)
+            + bias[slot]
+        )
 
     @pl.loop(0, n)
     def _(slot):
         @pl.when(slot <= me)
         def _():
-            @pl.when(slot >= 2)
+            @pl.when(~has_right)
             def _():
-                kv_wait(slot)
-
-            @pl.when((slot >= 2) & has_right)
-            def _():
-                kv_copy(slot).start()
-
-            attend(slot)
+                take(0, slot)
+
+            @pl.loop(0, heads // group)
+            def _(g):
+                keys = kv[0, slot, :, head_lanes(g)]
+                for member in range(group):
+                    h = g * group + member
+                    scores = scores_of(slot, h, keys)
+                    best = top[h]
+                    for t in range(0, length, 128):
+                        best = jnp.maximum(best, scores[:, t : t + 128])
+                    top[h] = best
 
     @pl.loop(0, heads)
     def _(h):
-        mine = pl.ds(pl.multiple_of(h * HEAD_DIM, HEAD_DIM), HEAD_DIM)
-        attended_ref[:, mine] = (acc[h] / jnp.sum(total[h], axis=1, keepdims=True)).astype(BF16)
+        top[h] = jnp.broadcast_to(jnp.max(top[h], axis=1, keepdims=True), top.shape[1:])
+
+    @pl.loop(0, n)
+    def _(slot):
+        @pl.when(slot <= me)
+        def _():
+            @pl.loop(0, heads // group)
+            def _(g):
+                keys = kv[0, slot, :, head_lanes(g)]
+                for member in range(group):
+                    h = g * group + member
+                    scores = scores_of(slot, h, keys)
+                    best = top[h]
+                    summed = total[h]
+                    for t in range(0, length, 128):
+                        part = jnp.exp2((scores[:, t : t + 128] - best) * scale)
+                        summed = summed + part
+                        weights[h, :, t : t + 128] = part.astype(BF16)
+                    total[h] = summed
+
+            @pl.when(~has_right)
+            def _():
+                take(1, slot)
+
+            @pl.loop(0, heads // group)
+            def _(g):
+                values = kv[1, slot, :, head_lanes(g)]
+                for member in range(group):
+                    h = g * group + member
+                    acc[h] += dot(weights[h], values)
+
+    @pl.loop(0, heads)
+    def _(h):
+        attended_ref[:, head_lanes(h)] = (
+            acc[h] / jnp.sum(total[h], axis=1, keepdims=True)
+        ).astype(BF16)
 
     @pl.loop(0, chunks)
     def _(j):
@@ -381,7 +430,8 @@
     def _(slot):
         @pl.when((slot <= me) & has_right)
         def _():
-            kv_copy(slot).wait_send()
+            pass_on(0, slot).wait_send()
+            pass_on(1, slot).wait_send()
 
 
 def on_device(
@@ -404,20 +454,21 @@
     heads = q_cols // HEAD_DIM
     per = CHUNK // HEAD_P
     kv_cols = key_states.shape[1]
-    skip = jnp.repeat(skip_gain, HEAD_P).reshape(1, channels)
     vmem = pl.BlockSpec(memory_space=pltpu.VMEM)
+    smem = pl.BlockSpec(memory_space=pltpu.SMEM)
     dma = pltpu.SemaphoreType.DMA
     out = jax.ShapeDtypeStruct((length, channels), BF16)
     return pl.pallas_call(
         functools.partial(kernel, n),
         out_shape=(out, jax.ShapeDtypeStruct((length, q_cols), BF16)),
-        in_specs=[pl.BlockSpec(memory_space=pltpu.SMEM)]
-        + [vmem] * 7
+        in_specs=[smem]
+        + [vmem] * 5
+        + [smem, vmem]
         + [pl.BlockSpec(memory_space=pl.ANY)]
         + [vmem] * 2,
         out_specs=(vmem, vmem),
         scratch_shapes=[
-            pltpu.VMEM((n, 2, length, kv_cols), BF16),
+            pltpu.VMEM((2, n, length, kv_cols), BF16),
             pltpu.VMEM((chunks, CHUNK, q_cols), BF16),
             pltpu.VMEM((chunks, CHUNK, q_cols), BF16),
             pltpu.VMEM((STATE, length), BF16),
@@ -432,12 +483,13 @@
             pltpu.VMEM((chunks, length, CHUNK), BF16),
             pltpu.VMEM((length, q_cols), F32),
             pltpu.VMEM((length, q_cols), BF16),
-            pltpu.VMEM((length, length), F32),
+            pltpu.VMEM((n, length, length), F32),
+            pltpu.VMEM((heads, length, length), BF16),
             pltpu.VMEM((heads, length, HEAD_DIM), F32),
             pltpu.VMEM((heads, length, HEAD_DIM), F32),
             pltpu.VMEM((heads, length, HEAD_DIM), F32),
-            dma((n,)),
-            dma((n + 1,)),
+            dma((2, n)),
+            dma((2, n + 1)),
             dma((chunks,)),
             dma((chunks,)),
             dma((chunks,)),
@@ -457,7 +509,7 @@
         output_map,
         step_size,
         log_decay,
-        skip,
+        skip_gain,
         norm_gain.reshape(1, channels),
         query_weight,
         key_states,

time: 101 us -> 77.4 us (0.77)
  Pallas kernels: 93.8 us -> 72 us
  local copies, waits for them, and re-layouts: 6.01 us -> 4.61 us
    pallas_call x1, Pallas kernels: 93.8 us -> 72 us  [on_device(): pl.pallas_call(functools.partial(kernel, n), out_shape=(out, jax.ShapeDty...]
where the time goes in v2:
time: 77.4 us; the launch traced here: 77.2 us
  Pallas kernels  72 us (93%)
  local copies, waits for them, and re-layouts  4.61 us (6%)
    pallas_call x1, Pallas kernels, on_device(): pl.pallas_call(functools.partial(kernel, n), out_shape=(out, jax.ShapeDty...  72 us
    unnamed x2, local copies, waits for them, and re-layouts  4.61 us

profile of v2, /device:TPU:26, one launch (start us, length us, event | category | flops | bytes accessed | tf_op | source)
XLA Modules:
  0.0 77.2 jit_solution(7655322773164295014)
XLA Ops:
  0.6 72.0 %mixer_attention.1 = (bf16[256,2048]{1,0:T(8,128)(2,1)}, bf16[256,2048]{1,0:T(8,128)(2,1)}) custom-call(s32[8,8]{1,0:T(8,128)} %mask_ref.1, bf16[256,2048]{1,0:T(8,128)(2,1)} %x_ref.1, bf16[256,128]{1,0:T(8,128)(2,1)} %b_ref.1, bf16[256,128]{1,0:T(8,128)(2,1)} %c_ref.1, f32[32,256]{1,0:T(8,128)} %dt_ref.1, f32[32,256]{1,0:T(8,128)} %ld_ref.1, f32[32]{0:T(128)} %skip_ref.1, ...), custom_call_target="tpu_custom_call" | custom-call | tf_op jit(solution)/shard_map/mixer_attention/pallas_call | solution.py:461
  72.6 2.3 %copy.15 = bf16[256,2048]{1,0:T(8,128)(2,1)} copy(bf16[256,2048]{1,0:T(8,128)(2,1)} %get-tuple-element.4) | data formatting | bytes 2097152
  74.9 2.3 %copy.16 = bf16[256,2048]{1,0:T(8,128)(2,1)} copy(bf16[256,2048]{1,0:T(8,128)(2,1)} %get-tuple-element.5) | data formatting | bytes 2097152

commit v3 on v2

--- a/solution.py
+++ b/solution.py
@@ -270,6 +270,10 @@
 
     half = length // 2
 
+    @pl.when(me >= 2)
+    def _():
+        take(0, 1)
+
     @pl.loop(0, chunks)
     def _(j):
         runs = col_run[j]
@@ -342,7 +346,9 @@
 
             @pl.loop(1, n)
             def _(slot, which=which):
-                take(which, slot)
+                @pl.when((which == 1) | (slot >= 2) | (me < 2))
+                def _():
+                    take(which, slot)
 
     q_all[...] = q_acc[...].astype(BF16)
     top[...] = jnp.full_like(top, NEGATIVE)
@@ -363,7 +369,7 @@
     def _(slot):
         @pl.when(slot <= me)
         def _():
-            @pl.when(~has_right)
+            @pl.when(~has_right & ((slot >= 2) | (me < 2)))
             def _():
                 take(0, slot)
 
@@ -432,6 +438,11 @@
         def _():
             pass_on(0, slot).wait_send()
             pass_on(1, slot).wait_send()
+
+
+def hand_on(mixer_ref, attended_ref, mixer_out, attended_out):
+    mixer_out[...] = mixer_ref[...]
+    attended_out[...] = attended_ref[...]
 
 
 def on_device(
@@ -458,7 +469,7 @@
     smem = pl.BlockSpec(memory_space=pltpu.SMEM)
     dma = pltpu.SemaphoreType.DMA
     out = jax.ShapeDtypeStruct((length, channels), BF16)
-    return pl.pallas_call(
+    results = pl.pallas_call(
         functools.partial(kernel, n),
         out_shape=(out, jax.ShapeDtypeStruct((length, q_cols), BF16)),
         in_specs=[smem]
@@ -515,6 +526,19 @@
         key_states,
         value_states,
     )
+    rows = length // 4
+    blocks = [
+        pl.BlockSpec((rows, channels), lambda i: (i, 0)),
+        pl.BlockSpec((rows, q_cols), lambda i: (i, 0)),
+    ]
+    return pl.pallas_call(
+        hand_on,
+        out_shape=(out, jax.ShapeDtypeStruct((length, q_cols), BF16)),
+        grid=(4,),
+        in_specs=blocks,
+        out_specs=blocks,
+        name="hand_on",
+    )(*results)
 
 
 def solution(mesh):

time: 77.4 us -> 74.3 us (0.960)
  local copies, waits for them, and re-layouts: 4.61 us -> 0 us
  Pallas kernels: 72 us -> 73.5 us
    unnamed x2 -> x0, local copies, waits for them, and re-layouts: 4.61 us -> none
    pallas_call x0 -> x1, Pallas kernels: none -> 3.75 us  [on_device(): pl.pallas_call(hand_on, out_shape=(out, jax.ShapeDtypeStruct((length, q_c...]
    pallas_call x1, Pallas kernels: 72 us -> 69.7 us  [on_device(): pl.pallas_call(functools.partial(kernel, n), out_shape=(out, jax.ShapeDty...]
where the time goes in v3:
time: 74.3 us; the launch traced here: 74.1 us
  Pallas kernels  73.5 us (99%)
    pallas_call x1, Pallas kernels, on_device(): pl.pallas_call(functools.partial(kernel, n), out_shape=(out, jax.ShapeDty...  69.7 us
    pallas_call x1, Pallas kernels, on_device(): pl.pallas_call(hand_on, out_shape=(out, jax.ShapeDtypeStruct((length, q_c...  3.75 us

profile of v3, /device:TPU:26, one launch (start us, length us, event | category | flops | bytes accessed | tf_op | source)
XLA Modules:
  0.0 74.1 jit_solution(2647478498907093019)
XLA Ops:
  0.6 69.7 %mixer_attention.1 = (bf16[256,2048]{1,0:T(8,128)(2,1)}, bf16[256,2048]{1,0:T(8,128)(2,1)}) custom-call(s32[8,8]{1,0:T(8,128)} %mask_ref.1, bf16[256,2048]{1,0:T(8,128)(2,1)} %x_ref.1, bf16[256,128]{1,0:T(8,128)(2,1)} %b_ref.1, bf16[256,128]{1,0:T(8,128)(2,1)} %c_ref.1, f32[32,256]{1,0:T(8,128)} %dt_ref.1, f32[32,256]{1,0:T(8,128)} %ld_ref.1, f32[32]{0:T(128)} %skip_ref.1, ...), custom_call_target="tpu_custom_call" | custom-call | tf_op jit(solution)/shard_map/mixer_attention/pallas_call | solution.py:472
  70.3 3.8 %hand_on.1 = (bf16[256,2048]{1,0:T(8,128)(2,1)}, bf16[256,2048]{1,0:T(8,128)(2,1)}) custom-call(bf16[256,2048]{1,0:T(8,128)(2,1)} %get-tuple-element.4.mixer_ref, bf16[256,2048]{1,0:T(8,128)(2,1)} %get-tuple-element.5.attended_ref), custom_call_target="tpu_custom_call" | custom-call | tf_op jit(solution)/shard_map/hand_on/pallas_call | solution.py:534
